TPU v7x, 256 devices: a whole 4x4x8 slice. The times are simulated.
256 devices in a mesh: seg: 8 (over x, y_hi), gx: 2 (over y_lo), gz: 16 (over z, core).
Axes of the slice: x: 4, y: 4 (y_hi: 2, y_lo: 2; y = y_hi * 2 + y_lo), z: 8, core: 2. Of those that a mesh axis runs over, the one named last changes fastest.
Arguments:
- terminal: float32 [8, 3, 128, 256, 256], P('seg', None, 'gx', 'gz'), may hold values from -6 to 6
- jump: float32 [8, 3, 128, 256, 256], P('seg', None, 'gx', 'gz'), may hold values from -61 to 61
- tangent: float32 [8, 3, 128, 256, 256], P('seg', None, 'gx', 'gz'), may hold values from -36 to 36
- base_velocity: float32 [256], replicated, may hold values from 0.5 to 2
- base_shear: float32 [256], replicated, may hold values from -2 to 2
Outputs:
- adjoint_field: float32 [8, 3, 128, 256, 256], P('seg', None, 'gx', 'gz')
All inputs are finite; a program needn't handle non-finite values. Where the computation divides by a largest or mean magnitude, that divisor is 1e-20 or more.
Results may differ from a plain program's by a relative error of at most 0.00018.
Values sent between devices are 32-bit elements; how exact they have to be, the bound alone decides.
A program may use at most 64 MiB of HBM per device.

v0:
```python
import jax
import jax.numpy as jnp
import numpy as np
from jax import lax
from jax.sharding import PartitionSpec as P

STEPS = 4
TIME_STEP = 0.15
DIFFUSE = 0.1
WALL_COEF = 0.0002
EPSILON = 1e-06
NEWTON_TURNS = 100


def with_halo(cells, sides, width):
    for axis, dim in sides:
        count = lax.axis_size(axis)
        head = lax.slice_in_dim(cells, 0, width, axis=dim)
        tail = lax.slice_in_dim(cells, cells.shape[dim] - width, cells.shape[dim], axis=dim)
        cells = jnp.concatenate(
            [
                lax.ppermute(tail, axis, [(i, (i + 1) % count) for i in range(count)]),
                cells,
                lax.ppermute(head, axis, [((i + 1) % count, i) for i in range(count)]),
            ],
            axis=dim,
        )
    return cells


def from_behind(value, axis, steps):
    count = lax.axis_size(axis)
    pairs = [(source, (source + steps) % count) for source in range(count)]
    return lax.ppermute(value, axis, pairs)


def invert_newton(matrix):
    order = matrix.shape[0]
    identity = np.eye(order)
    scale_one = np.max(np.sum(np.abs(matrix), axis=0))
    scale_inf = np.max(np.sum(np.abs(matrix), axis=1))
    approx = matrix.T / (scale_one * scale_inf)
    for turn_index in range(NEWTON_TURNS):
        approx = approx @ (2.0 * identity - matrix @ approx)
    return approx


def wall_table(points):
    intervals = points - 1
    cheb_nodes = np.cos(np.pi * np.arange(points) / intervals)
    weights = np.ones(points)
    weights[0] = 2.0
    weights[-1] = 2.0
    weights = weights * (-1.0) ** np.arange(points)
    spread = cheb_nodes[:, None] - cheb_nodes[None, :]
    first_deriv = weights[:, None] / weights[None, :] / (spread + np.eye(points))
    first_deriv = first_deriv - np.eye(points) * first_deriv.sum(axis=1)[:, None]
    second = first_deriv @ first_deriv
    interior = np.eye(points - 2) - WALL_COEF * second[1:-1, 1:-1]
    helm_table = np.zeros((points, points))
    helm_table[1:-1, 1:-1] = invert_newton(interior)
    return jnp.asarray(helm_table.T, dtype=jnp.float32)


def advance(padded, velocity, shear, table_t):
    center = padded[:, 2:-2, 2:-2, :]
    fwd2_x = padded[:, 4:, 2:-2, :]
    fwd1_x = padded[:, 3:-1, 2:-2, :]
    back1_x = padded[:, 1:-3, 2:-2, :]
    back2_x = padded[:, :-4, 2:-2, :]
    fwd2_z = padded[:, 2:-2, 4:, :]
    fwd1_z = padded[:, 2:-2, 3:-1, :]
    back1_z = padded[:, 2:-2, 1:-3, :]
    back2_z = padded[:, 2:-2, :-4, :]
    advect = (back2_x - fwd2_x + 8.0 * (fwd1_x - back1_x)) / 12.0
    lap_x = (16.0 * (fwd1_x + back1_x) - (fwd2_x + back2_x) - 30.0 * center) / 12.0
    lap_z = (16.0 * (fwd1_z + back1_z) - (fwd2_z + back2_z) - 30.0 * center) / 12.0
    explicit = center + TIME_STEP * velocity * advect + DIFFUSE * (lap_x + lap_z)
    explicit = jnp.concatenate(
        [explicit[:1], explicit[1:2] - TIME_STEP * shear * center[:1], explicit[2:]], axis=0
    )
    flattened = explicit.reshape(-1, explicit.shape[-1])
    updated = jnp.dot(
        flattened, table_t, precision=lax.Precision.HIGHEST, preferred_element_type=jnp.float32
    )
    return updated.reshape(explicit.shape)


def extend(adjoint, width):
    along_x = with_halo(adjoint, (("gx", 1),), width)
    return with_halo(along_x, (("gz", 2),), width)


def shards(terminal, jump, tangent, base_velocity, base_shear):
    table_t = wall_table(base_velocity.shape[0])
    received = from_behind(terminal, "seg", -1)
    started = received[0] + jump[0]
    direction = tangent[0]
    products = lax.psum(
        (jnp.sum(started * direction), jnp.sum(direction * direction)), ("gx", "gz")
    )
    along_coef = products[0] / (products[1] + EPSILON)
    adjoint = started - along_coef * direction
    for step_index in range(STEPS):
        padded = extend(adjoint, 2)
        adjoint = advance(padded, base_velocity, base_shear, table_t)
    return adjoint[None]


def solution(mesh):
    in_specs = (
        P("seg", None, "gx", "gz", None),
        P("seg", None, "gx", "gz", None),
        P("seg", None, "gx", "gz", None),
        P(),
        P(),
    )
    out_specs = P("seg", None, "gx", "gz", None)
    return jax.shard_map(shards, mesh=mesh, in_specs=in_specs, out_specs=out_specs, check_vma=False)
```

profile of v0, /device:TPU:22, one launch (start us, length us, event | category | flops | bytes accessed | tf_op | source)
XLA Modules:
  0.0 248.8 jit_solution(7663834592041668082)
XLA Ops:
  0.0 0.3 collective-permute-start
  0.3 73.3 %collective-permute-done = f32[1,3,64,16,256]{4,3,2,1,0:T(8,128)S(1)} collective-permute-done((f32[1,3,64,16,256]{4,3,2,1,0:T(8,128)}, f32[1,3,64,16,256]{4,3,2,1,0:T(8,128)S(1)}, u32[]{:S(2)}, u32[]{:S(2)}) %collective-permute-start) | collective-permute-done | bytes 3145760 | tf_op jit(solution)/shard_map/ppermute | solution.py:34
  73.7 5.4 %fusion.39 = (f32[]{:T(128)}, f32[]{:T(128)}) fusion(f32[1,3,64,16,256]{4,3,2,1,0:T(8,128)} %param.8, f32[1,3,64,16,256]{4,3,2,1,0:T(8,128)S(1)} %collective-permute-done, f32[1,3,64,16,256]{4,3,2,1,0:T(8,128)} %param.7), kind=kLoop, calls=%fused_computation.85 | loop fusion | flops 3932158 | bytes 9437192 | tf_op jit(solution)/shard_map/reduce_sum | solution.py:100
  79.1 58.7 %all-reduce = (f32[]{:T(128)}, f32[]{:T(128)}) all-reduce(f32[]{:T(128)} %get-tuple-element.6, f32[]{:T(128)} %get-tuple-element.5), channel_id=1, replica_groups=mesh['seg'=8,'gx'=2,'gz'=16] {'gx','gz'}, use_global_device_ids=true, to_apply=%region_1.0 | all-reduce | flops 2 | bytes 16 | tf_op jit(solution)/shard_map/psum | solution.py:99
  139.2 4.0 %fusion.40 = f32[3,64,16,256]{3,2,1,0:T(8,128)S(1)} fusion(f32[1,3,64,16,256]{4,3,2,1,0:T(8,128)S(1)} %copy-done, f32[]{:T(128)S(6)} %div.31, f32[1,3,64,16,256]{4,3,2,1,0:T(8,128)} %copy-done.1, f32[1,3,64,16,256]{4,3,2,1,0:T(8,128)} %param.7), kind=kLoop, calls=%fused_computation.86 | loop fusion | flops 2359296 | bytes 12582916 | tf_op jit(solution)/shard_map/sub | solution.py:103
  143.2 0.8 collective-permute-start.1
  144.0 1.3 collective-permute-start.2
  145.3 2.6 %collective-permute-done.1 = f32[3,2,16,256]{3,2,1,0:T(8,128)S(1)} collective-permute-done((f32[3,2,16,256]{3,2,1,0:T(8,128)S(1)}, f32[3,2,16,256]{3,2,1,0:T(8,128)S(1)}, u32[]{:S(2)}, u32[]{:S(2)}) %collective-permute-start.1) | collective-permute-done | bytes 98336 | tf_op jit(solution)/shard_map/ppermute | solution.py:22
  147.9 1.1 collective-permute-done.2
  149.0 0.3 pad_maximum_fusion.26
  149.3 0.0 collective-permute-start.3
  149.3 0.5 collective-permute-start.4
  149.8 5.0 %collective-permute-done.3 = f32[3,68,2,256]{3,2,1,0:T(2,128)S(1)} collective-permute-done((f32[3,68,2,256]{3,2,1,0:T(2,128)S(1)}, f32[3,68,2,256]{3,2,1,0:T(2,128)S(1)}, u32[]{:S(2)}, u32[]{:S(2)}) %collective-permute-start.3) | collective-permute-done | bytes 417824 | tf_op jit(solution)/shard_map/ppermute | solution.py:24
  154.8 3.1 %collective-permute-done.4 = f32[3,68,2,256]{3,2,1,0:T(2,128)S(1)} collective-permute-done((f32[3,68,2,256]{3,2,1,0:T(2,128)S(1)}, f32[3,68,2,256]{3,2,1,0:T(2,128)S(1)}, u32[]{:S(2)}, u32[]{:S(2)}) %collective-permute-start.4) | collective-permute-done | bytes 417824 | tf_op jit(solution)/shard_map/ppermute | solution.py:22
  158.0 1.3 pad_maximum_fusion
  159.3 4.1 %fusion.30 = f32[3,64,16,256]{3,2,1,0:T(8,128)} fusion(f32[3,68,18,256]{3,2,1,0:T(8,128)S(1)} %get-tuple-element.22, f32[3,68,18,256]{3,2,1,0:T(8,128)S(1)} %get-tuple-element.21, f32[3,64,16,256]{3,2,1,0:T(8,128)S(1)} %fusion.40, f32[3,2,16,256]{3,2,1,0:T(8,128)S(1)} %collective-permute-done.2, f32[3,2,16,256]{3,2,1,0:T(8,128)S(1)} %collective-permute-done.1, ...), kind=kLoop, calls=%fused_computation.67 | loop fusion | flops 18874368 | bytes 19072000 | tf_op jit(solution)/shard_map/add | solution.py:78
  163.4 2.3 fusion.52
  165.7 0.3 pad_maximum_fusion.12
  166.0 0.6 copy-done.2
  166.7 2.6 %fusion.54 = f32[3072,256]{1,0:T(8,128)S(1)} fusion(f32[3072,256]{1,0:T(8,128)S(1)} %bitcast.47, f32[256,256]{1,0:T(8,128)S(1)} %copy-done.2), kind=kOutput, calls=%fused_computation.116 | convolution fusion | flops 2415919104 | bytes 6553600 | tf_op jit(solution)/shard_map/dot_general | solution.py:83
  169.3 1.1 collective-permute-start.5
  170.4 1.1 collective-permute-start.6
  171.4 2.6 %collective-permute-done.5 = f32[3,2,16,256]{3,2,1,0:T(8,128)S(1)} collective-permute-done((f32[3,2,16,256]{3,2,1,0:T(8,128)S(1)}, f32[3,2,16,256]{3,2,1,0:T(8,128)S(1)}, u32[]{:S(2)}, u32[]{:S(2)}) %collective-permute-start.5) | collective-permute-done | bytes 98336 | tf_op jit(solution)/shard_map/ppermute | solution.py:22
  174.0 1.1 collective-permute-done.6
  175.1 0.3 pad_maximum_fusion.23
  175.4 0.0 collective-permute-start.7
  175.4 0.5 collective-permute-start.8
  175.9 0.1 slice.326
  176.0 5.0 %collective-permute-done.7 = f32[3,68,2,256]{3,2,1,0:T(2,128)S(1)} collective-permute-done((f32[3,68,2,256]{3,2,1,0:T(2,128)S(1)}, f32[3,68,2,256]{3,2,1,0:T(2,128)S(1)}, u32[]{:S(2)}, u32[]{:S(2)}) %collective-permute-start.7) | collective-permute-done | bytes 417824 | tf_op jit(solution)/shard_map/ppermute | solution.py:24
  181.0 3.1 %collective-permute-done.8 = f32[3,68,2,256]{3,2,1,0:T(2,128)S(1)} collective-permute-done((f32[3,68,2,256]{3,2,1,0:T(2,128)S(1)}, f32[3,68,2,256]{3,2,1,0:T(2,128)S(1)}, u32[]{:S(2)}, u32[]{:S(2)}) %collective-permute-start.8) | collective-permute-done | bytes 417824 | tf_op jit(solution)/shard_map/ppermute | solution.py:22
  184.1 1.3 pad_maximum_fusion.1
  185.4 5.0 %fusion.24 = f32[3,64,16,256]{3,2,1,0:T(8,128)} fusion(f32[3,68,18,256]{3,2,1,0:T(8,128)S(1)} %get-tuple-element.18, f32[3,68,18,256]{3,2,1,0:T(8,128)S(1)} %get-tuple-element.17, f32[3,64,16,256]{3,2,1,0:T(8,128)S(1)} %bitcast.41, f32[3,2,16,256]{3,2,1,0:T(8,128)} %copy-done.3, f32[3,2,16,256]{3,2,1,0:T(8,128)S(1)} %collective-permute-done.5, ...), kind=kLoop, calls=%fused_computation.57 | loop fusion | flops 18874368 | bytes 19072000 | tf_op jit(solution)/shard_map/add | solution.py:78
  190.4 2.3 fusion.50
  192.7 0.3 pad_maximum_fusion.13
  193.0 2.6 %fusion.55 = f32[3072,256]{1,0:T(8,128)S(1)} fusion(f32[3072,256]{1,0:T(8,128)S(1)} %bitcast.48, f32[256,256]{1,0:T(8,128)S(1)} %copy-done.2), kind=kOutput, calls=%fused_computation.117 | convolution fusion | flops 2415919104 | bytes 6553600 | tf_op jit(solution)/shard_map/dot_general | solution.py:83
  195.7 1.1 collective-permute-start.10
  196.8 1.1 collective-permute-start.9
  197.8 2.6 %collective-permute-done.10 = f32[3,2,16,256]{3,2,1,0:T(8,128)S(1)} collective-permute-done((f32[3,2,16,256]{3,2,1,0:T(8,128)S(1)}, f32[3,2,16,256]{3,2,1,0:T(8,128)S(1)}, u32[]{:S(2)}, u32[]{:S(2)}) %collective-permute-start.10) | collective-permute-done | bytes 98336 | tf_op jit(solution)/shard_map/ppermute | solution.py:24
  200.4 1.1 collective-permute-done.9
  201.4 0.3 pad_maximum_fusion.20
  201.7 0.0 collective-permute-start.11
  201.8 0.5 collective-permute-start.12
  202.3 0.1 slice.340
  202.3 5.0 %collective-permute-done.11 = f32[3,68,2,256]{3,2,1,0:T(2,128)S(1)} collective-permute-done((f32[3,68,2,256]{3,2,1,0:T(2,128)S(1)}, f32[3,68,2,256]{3,2,1,0:T(2,128)S(1)}, u32[]{:S(2)}, u32[]{:S(2)}) %collective-permute-start.11) | collective-permute-done | bytes 417824 | tf_op jit(solution)/shard_map/ppermute | solution.py:24
  207.3 3.1 %collective-permute-done.12 = f32[3,68,2,256]{3,2,1,0:T(2,128)S(1)} collective-permute-done((f32[3,68,2,256]{3,2,1,0:T(2,128)S(1)}, f32[3,68,2,256]{3,2,1,0:T(2,128)S(1)}, u32[]{:S(2)}, u32[]{:S(2)}) %collective-permute-start.12) | collective-permute-done | bytes 417824 | tf_op jit(solution)/shard_map/ppermute | solution.py:22
  210.5 1.3 pad_maximum_fusion.2
  211.8 4.9 %fusion.18 = f32[3,64,16,256]{3,2,1,0:T(8,128)} fusion(f32[3,68,18,256]{3,2,1,0:T(8,128)S(1)} %get-tuple-element.14, f32[3,68,18,256]{3,2,1,0:T(8,128)S(1)} %get-tuple-element.13, f32[3,64,16,256]{3,2,1,0:T(8,128)S(1)} %bitcast.45, f32[3,2,16,256]{3,2,1,0:T(8,128)S(1)} %collective-permute-done.10, f32[3,2,16,256]{3,2,1,0:T(8,128)} %copy-done.4, ...), kind=kLoop, calls=%fused_computation.47 | loop fusion | flops 18874368 | bytes 19072000 | tf_op jit(solution)/shard_map/add | solution.py:78
  216.6 2.3 fusion.48
  219.0 0.3 pad_maximum_fusion.14
  219.3 2.6 %fusion.56 = f32[3072,256]{1,0:T(8,128)S(1)} fusion(f32[3072,256]{1,0:T(8,128)S(1)} %bitcast.46, f32[256,256]{1,0:T(8,128)S(1)} %copy-done.2), kind=kOutput, calls=%fused_computation.118 | convolution fusion | flops 2415919104 | bytes 6553600 | tf_op jit(solution)/shard_map/dot_general | solution.py:83
  221.9 1.1 collective-permute-start.13
  223.0 1.0 collective-permute-start.14
  224.1 2.6 %collective-permute-done.13 = f32[3,2,16,256]{3,2,1,0:T(8,128)S(1)} collective-permute-done((f32[3,2,16,256]{3,2,1,0:T(8,128)S(1)}, f32[3,2,16,256]{3,2,1,0:T(8,128)S(1)}, u32[]{:S(2)}, u32[]{:S(2)}) %collective-permute-start.13) | collective-permute-done | bytes 98336 | tf_op jit(solution)/shard_map/ppermute | solution.py:22
  226.7 1.1 collective-permute-done.14
  227.7 0.3 pad_maximum_fusion.17
  228.0 0.0 collective-permute-start.15
  228.0 0.5 collective-permute-start.16
  228.5 0.1 slice.354
  228.6 5.0 %collective-permute-done.15 = f32[3,68,2,256]{3,2,1,0:T(2,128)S(1)} collective-permute-done((f32[3,68,2,256]{3,2,1,0:T(2,128)S(1)}, f32[3,68,2,256]{3,2,1,0:T(2,128)S(1)}, u32[]{:S(2)}, u32[]{:S(2)}) %collective-permute-start.15) | collective-permute-done | bytes 417824 | tf_op jit(solution)/shard_map/ppermute | solution.py:24
  233.6 3.1 %collective-permute-done.16 = f32[3,68,2,256]{3,2,1,0:T(2,128)S(1)} collective-permute-done((f32[3,68,2,256]{3,2,1,0:T(2,128)S(1)}, f32[3,68,2,256]{3,2,1,0:T(2,128)S(1)}, u32[]{:S(2)}, u32[]{:S(2)}) %collective-permute-start.16) | collective-permute-done | bytes 417824 | tf_op jit(solution)/shard_map/ppermute | solution.py:22
  236.7 1.3 pad_maximum_fusion.3
  238.0 4.1 %fusion.12 = f32[3,64,16,256]{3,2,1,0:T(8,128)} fusion(f32[3,68,18,256]{3,2,1,0:T(8,128)S(1)} %get-tuple-element.10, f32[3,68,18,256]{3,2,1,0:T(8,128)S(1)} %get-tuple-element.9, f32[3,64,16,256]{3,2,1,0:T(8,128)S(1)} %bitcast.37, f32[3,2,16,256]{3,2,1,0:T(8,128)S(1)} %collective-permute-done.14, f32[3,2,16,256]{3,2,1,0:T(8,128)S(1)} %collective-permute-done.13, ...), kind=kLoop, calls=%fused_computation.37 | loop fusion | flops 18874368 | bytes 19072000 | tf_op jit(solution)/shard_map/add | solution.py:78
  242.1 2.4 fusion.46
  244.5 4.3 %fusion.41 = f32[1,3,64,16,256]{4,3,2,1,0:T(8,128)} fusion(f32[256,256,1,1]{1,0,3,2:T(8,128)S(1)} %copy-done.5, f32[1,64,16,256]{3,2,1,0:T(8,128)S(1)} %get-tuple-element.26, f32[1,64,16,256]{3,2,1,0:T(8,128)S(1)} %get-tuple-element.27, f32[1,64,16,256]{3,2,1,0:T(8,128)S(1)} %get-tuple-element.25), kind=kOutput, calls=%fused_computation.87 | convolution fusion | flops 2417491968 | bytes 6553600 | tf_op jit(solution)/shard_map/dot_general | solution.py:83
  (21 shorter events, 0.1 us)
Async XLA Ops:
  0.0 139.1 %copy-start = (f32[1,3,64,16,256]{4,3,2,1,0:T(8,128)S(1)}, f32[1,3,64,16,256]{4,3,2,1,0:T(8,128)}, u32[]{:S(2)}) copy-start(f32[1,3,64,16,256]{4,3,2,1,0:T(8,128)} %param.8) | copy-start | bytes 9437188
  0.0 73.7 %collective-permute-start = (f32[1,3,64,16,256]{4,3,2,1,0:T(8,128)}, f32[1,3,64,16,256]{4,3,2,1,0:T(8,128)S(1)}, u32[]{:S(2)}, u32[]{:S(2)}) collective-permute-start(f32[1,3,64,16,256]{4,3,2,1,0:T(8,128)} %param.6), channel_id=1, source_target_pairs={{0,224},{32,0},{64,32},{96,64},{128,96},{160,128},{192,160},{224,1... | collective-permute-start | bytes 9437192 | tf_op jit(solution)/shard_map/ppermute | solution.py:34
  73.7 5.4 %copy-start.1 = (f32[1,3,64,16,256]{4,3,2,1,0:T(8,128)}, f32[1,3,64,16,256]{4,3,2,1,0:T(8,128)S(1)}, u32[]{:S(2)}) copy-start(f32[1,3,64,16,256]{4,3,2,1,0:T(8,128)S(1)} %collective-permute-done) | copy-start | bytes 9437188
  143.2 6.6 %copy-start.6 = (f32[256]{0:T(256)S(1)}, f32[256]{0:T(256)}, u32[]{:S(2)}) copy-start(f32[256]{0:T(256)} %param.9) | copy-start | bytes 3076
  143.2 6.6 %copy-start.7 = (f32[256]{0:T(256)S(1)}, f32[256]{0:T(256)}, u32[]{:S(2)}) copy-start(f32[256]{0:T(256)} %param.10) | copy-start | bytes 3076
  143.2 4.7 %collective-permute-start.1 = (f32[3,2,16,256]{3,2,1,0:T(8,128)S(1)}, f32[3,2,16,256]{3,2,1,0:T(8,128)S(1)}, u32[]{:S(2)}, u32[]{:S(2)}) collective-permute-start(f32[3,2,16,256]{3,2,1,0:T(8,128)S(1)} %get-tuple-element.43), channel_id=1, source_target_pairs={{0,16},{16,0},{1,17},{17,1},{2,18},{18,2},{3,19},{19,3},{4,20},{20... | collective-permute-start | bytes 294920 | tf_op jit(solution)/shard_map/ppermute | solution.py:22
  144.0 4.9 %collective-permute-start.2 = (f32[3,2,16,256]{3,2,1,0:T(8,128)S(1)}, f32[3,2,16,256]{3,2,1,0:T(8,128)S(1)}, u32[]{:S(2)}, u32[]{:S(2)}) collective-permute-start(f32[3,2,16,256]{3,2,1,0:T(8,128)S(1)} %get-tuple-element.44), channel_id=1, source_target_pairs={{16,0},{0,16},{17,1},{1,17},{18,2},{2,18},{19,3},{3,19},{20,4},{4,... | collective-permute-start | bytes 294920 | tf_op jit(solution)/shard_map/ppermute | solution.py:24
  149.3 5.6 %collective-permute-start.3 = (f32[3,68,2,256]{3,2,1,0:T(2,128)S(1)}, f32[3,68,2,256]{3,2,1,0:T(2,128)S(1)}, u32[]{:S(2)}, u32[]{:S(2)}) collective-permute-start(f32[3,68,2,256]{3,2,1,0:T(2,128)S(1)} %get-tuple-element.23), channel_id=1, source_target_pairs={{1,0},{2,1},{3,2},{4,3},{5,4},{6,5},{7,6},{8,7},{9,8},{10,9},{11,1... | collective-permute-start | bytes 1253384 | tf_op jit(solution)/shard_map/ppermute | solution.py:24
  149.3 8.7 %collective-permute-start.4 = (f32[3,68,2,256]{3,2,1,0:T(2,128)S(1)}, f32[3,68,2,256]{3,2,1,0:T(2,128)S(1)}, u32[]{:S(2)}, u32[]{:S(2)}) collective-permute-start(f32[3,68,2,256]{3,2,1,0:T(2,128)S(1)} %get-tuple-element.24), channel_id=1, source_target_pairs={{0,1},{1,2},{2,3},{3,4},{4,5},{5,6},{6,7},{7,8},{8,9},{9,10},{10,1... | collective-permute-start | bytes 1253384 | tf_op jit(solution)/shard_map/ppermute | solution.py:22
  165.7 1.0 copy-start.2
  169.3 4.7 %collective-permute-start.5 = (f32[3,2,16,256]{3,2,1,0:T(8,128)S(1)}, f32[3,2,16,256]{3,2,1,0:T(8,128)S(1)}, u32[]{:S(2)}, u32[]{:S(2)}) collective-permute-start(f32[3,2,16,256]{3,2,1,0:T(8,128)S(1)} %get-tuple-element.38), channel_id=1, source_target_pairs={{0,16},{16,0},{1,17},{17,1},{2,18},{18,2},{3,19},{19,3},{4,20},{20... | collective-permute-start | bytes 294920 | tf_op jit(solution)/shard_map/ppermute | solution.py:22
  170.4 4.7 %collective-permute-start.6 = (f32[3,2,16,256]{3,2,1,0:T(8,128)S(1)}, f32[3,2,16,256]{3,2,1,0:T(8,128)S(1)}, u32[]{:S(2)}, u32[]{:S(2)}) collective-permute-start(f32[3,2,16,256]{3,2,1,0:T(8,128)S(1)} %get-tuple-element.39), channel_id=1, source_target_pairs={{16,0},{0,16},{17,1},{1,17},{18,2},{2,18},{19,3},{3,19},{20,4},{4,... | collective-permute-start | bytes 294920 | tf_op jit(solution)/shard_map/ppermute | solution.py:24
  175.1 10.3 %copy-start.3 = (f32[3,2,16,256]{3,2,1,0:T(8,128)}, f32[3,2,16,256]{3,2,1,0:T(8,128)S(1)}, u32[]{:S(2)}) copy-start(f32[3,2,16,256]{3,2,1,0:T(8,128)S(1)} %collective-permute-done.6) | copy-start | bytes 294916
  175.4 5.6 %collective-permute-start.7 = (f32[3,68,2,256]{3,2,1,0:T(2,128)S(1)}, f32[3,68,2,256]{3,2,1,0:T(2,128)S(1)}, u32[]{:S(2)}, u32[]{:S(2)}) collective-permute-start(f32[3,68,2,256]{3,2,1,0:T(2,128)S(1)} %get-tuple-element.19), channel_id=1, source_target_pairs={{1,0},{2,1},{3,2},{4,3},{5,4},{6,5},{7,6},{8,7},{9,8},{10,9},{11,1... | collective-permute-start | bytes 1253384 | tf_op jit(solution)/shard_map/ppermute | solution.py:24
  175.4 8.7 %collective-permute-start.8 = (f32[3,68,2,256]{3,2,1,0:T(2,128)S(1)}, f32[3,68,2,256]{3,2,1,0:T(2,128)S(1)}, u32[]{:S(2)}, u32[]{:S(2)}) collective-permute-start(f32[3,68,2,256]{3,2,1,0:T(2,128)S(1)} %get-tuple-element.20), channel_id=1, source_target_pairs={{0,1},{1,2},{2,3},{3,4},{4,5},{5,6},{6,7},{7,8},{8,9},{9,10},{10,1... | collective-permute-start | bytes 1253384 | tf_op jit(solution)/shard_map/ppermute | solution.py:22
  195.7 4.7 %collective-permute-start.10 = (f32[3,2,16,256]{3,2,1,0:T(8,128)S(1)}, f32[3,2,16,256]{3,2,1,0:T(8,128)S(1)}, u32[]{:S(2)}, u32[]{:S(2)}) collective-permute-start(f32[3,2,16,256]{3,2,1,0:T(8,128)S(1)} %get-tuple-element.34), channel_id=1, source_target_pairs={{16,0},{0,16},{17,1},{1,17},{18,2},{2,18},{19,3},{3,19},{20,4},{4,... | collective-permute-start | bytes 294920 | tf_op jit(solution)/shard_map/ppermute | solution.py:24
  196.8 4.7 %collective-permute-start.9 = (f32[3,2,16,256]{3,2,1,0:T(8,128)S(1)}, f32[3,2,16,256]{3,2,1,0:T(8,128)S(1)}, u32[]{:S(2)}, u32[]{:S(2)}) collective-permute-start(f32[3,2,16,256]{3,2,1,0:T(8,128)S(1)} %get-tuple-element.33), channel_id=1, source_target_pairs={{0,16},{16,0},{1,17},{17,1},{2,18},{18,2},{3,19},{19,3},{4,20},{20... | collective-permute-start | bytes 294920 | tf_op jit(solution)/shard_map/ppermute | solution.py:22
  201.4 10.3 %copy-start.4 = (f32[3,2,16,256]{3,2,1,0:T(8,128)}, f32[3,2,16,256]{3,2,1,0:T(8,128)S(1)}, u32[]{:S(2)}) copy-start(f32[3,2,16,256]{3,2,1,0:T(8,128)S(1)} %collective-permute-done.9) | copy-start | bytes 294916
  201.7 5.6 %collective-permute-start.11 = (f32[3,68,2,256]{3,2,1,0:T(2,128)S(1)}, f32[3,68,2,256]{3,2,1,0:T(2,128)S(1)}, u32[]{:S(2)}, u32[]{:S(2)}) collective-permute-start(f32[3,68,2,256]{3,2,1,0:T(2,128)S(1)} %get-tuple-element.15), channel_id=1, source_target_pairs={{1,0},{2,1},{3,2},{4,3},{5,4},{6,5},{7,6},{8,7},{9,8},{10,9},{11,1... | collective-permute-start | bytes 1253384 | tf_op jit(solution)/shard_map/ppermute | solution.py:24
  201.8 8.7 %collective-permute-start.12 = (f32[3,68,2,256]{3,2,1,0:T(2,128)S(1)}, f32[3,68,2,256]{3,2,1,0:T(2,128)S(1)}, u32[]{:S(2)}, u32[]{:S(2)}) collective-permute-start(f32[3,68,2,256]{3,2,1,0:T(2,128)S(1)} %get-tuple-element.16), channel_id=1, source_target_pairs={{0,1},{1,2},{2,3},{3,4},{4,5},{5,6},{6,7},{7,8},{8,9},{9,10},{10,1... | collective-permute-start | bytes 1253384 | tf_op jit(solution)/shard_map/ppermute | solution.py:22
  221.9 4.7 %collective-permute-start.13 = (f32[3,2,16,256]{3,2,1,0:T(8,128)S(1)}, f32[3,2,16,256]{3,2,1,0:T(8,128)S(1)}, u32[]{:S(2)}, u32[]{:S(2)}) collective-permute-start(f32[3,2,16,256]{3,2,1,0:T(8,128)S(1)} %get-tuple-element.28), channel_id=1, source_target_pairs={{0,16},{16,0},{1,17},{17,1},{2,18},{18,2},{3,19},{19,3},{4,20},{20... | collective-permute-start | bytes 294920 | tf_op jit(solution)/shard_map/ppermute | solution.py:22
  223.0 4.7 %collective-permute-start.14 = (f32[3,2,16,256]{3,2,1,0:T(8,128)S(1)}, f32[3,2,16,256]{3,2,1,0:T(8,128)S(1)}, u32[]{:S(2)}, u32[]{:S(2)}) collective-permute-start(f32[3,2,16,256]{3,2,1,0:T(8,128)S(1)} %get-tuple-element.29), channel_id=1, source_target_pairs={{16,0},{0,16},{17,1},{1,17},{18,2},{2,18},{19,3},{3,19},{20,4},{4,... | collective-permute-start | bytes 294920 | tf_op jit(solution)/shard_map/ppermute | solution.py:24
  228.0 5.6 %collective-permute-start.15 = (f32[3,68,2,256]{3,2,1,0:T(2,128)S(1)}, f32[3,68,2,256]{3,2,1,0:T(2,128)S(1)}, u32[]{:S(2)}, u32[]{:S(2)}) collective-permute-start(f32[3,68,2,256]{3,2,1,0:T(2,128)S(1)} %get-tuple-element.11), channel_id=1, source_target_pairs={{1,0},{2,1},{3,2},{4,3},{5,4},{6,5},{7,6},{8,7},{9,8},{10,9},{11,1... | collective-permute-start | bytes 1253384 | tf_op jit(solution)/shard_map/ppermute | solution.py:24
  228.0 8.7 %collective-permute-start.16 = (f32[3,68,2,256]{3,2,1,0:T(2,128)S(1)}, f32[3,68,2,256]{3,2,1,0:T(2,128)S(1)}, u32[]{:S(2)}, u32[]{:S(2)}) collective-permute-start(f32[3,68,2,256]{3,2,1,0:T(2,128)S(1)} %get-tuple-element.12), channel_id=1, source_target_pairs={{0,1},{1,2},{2,3},{3,4},{4,5},{5,6},{6,7},{7,8},{8,9},{9,10},{10,1... | collective-permute-start | bytes 1253384 | tf_op jit(solution)/shard_map/ppermute | solution.py:22
  242.1 2.4 copy-start.5
where the time goes:
time: 249 us
  waiting for transfers between devices  120 us (48%)
  blocking collectives  58.7 us (24%)
  other arithmetic  44.1 us (18%)
  matrix products  12.1 us (5%)
  starting transfers between devices  10.8 us (4%)
    ppermute x1, waiting for transfers between devices, from_behind(): return lax.ppermute(value, axis, pairs)  73.3 us
    psum x1, blocking collectives, shards(): lax.psum((jnp.sum(started * direction), jnp.sum(direction * direction)),...  58.7 us
    ppermute x8, waiting for transfers between devices, with_halo(): lax.ppermute(head, axis, [((i + 1) % count, i) for i in range(count)])  25.7 us
    ppermute x8, waiting for transfers between devices, with_halo(): lax.ppermute(tail, axis, [(i, (i + 1) % count) for i in range(count)])  21.4 us
    add x4, other arithmetic, advance(): center + TIME_STEP * velocity * advect + DIFFUSE * (lap_x + lap_z)  18 us
    dot_general x4, matrix products, advance(): jnp.dot(flattened, table_t, precision=lax.Precision.HIGHEST, preferred_el...  12.1 us
    slice x4, other arithmetic, advance(): explicit[:1]  9.38 us
    ppermute x8, starting transfers between devices, with_halo(): lax.ppermute(tail, axis, [(i, (i + 1) % count) for i in range(count)])  5.99 us
  transfers between devices with their start and end apart: 17, of which 17 were waited for; matrix products, arithmetic and copies ran while one was open for 0% of the time, Pallas kernels for 0%

commit v1 on v0

--- a/solution.py
+++ b/solution.py
@@ -97,7 +97,7 @@
     started = received[0] + jump[0]
     direction = tangent[0]
     products = lax.psum(
-        (jnp.sum(started * direction), jnp.sum(direction * direction)), ("gx", "gz")
+        lax.psum((jnp.sum(started * direction), jnp.sum(direction * direction)), "gz"), "gx"
     )
     along_coef = products[0] / (products[1] + EPSILON)
     adjoint = started - along_coef * direction

time: 249 us -> 225 us (0.904)
  blocking collectives: 58.7 us -> 34.2 us
    psum x1, blocking collectives: 58.7 us -> 28.6 us  [shards(): lax.psum((jnp.sum(started * direction), jnp.sum(direction * direction)),...]
    psum x0 -> x1, blocking collectives: none -> 5.58 us  [shards(): lax.psum(lax.psum((jnp.sum(started * direction), jnp.sum(direction * dire...]
where the time goes in v1:
time: 225 us
  waiting for transfers between devices  121 us (54%)
  other arithmetic  44.1 us (20%)
  blocking collectives  34.2 us (15%)
  matrix products  12.1 us (5%)
  starting transfers between devices  10.8 us (5%)
    ppermute x1, waiting for transfers between devices, from_behind(): return lax.ppermute(value, axis, pairs)  73.3 us
    psum x1, blocking collectives, shards(): lax.psum((jnp.sum(started * direction), jnp.sum(direction * direction)),...  28.6 us
    ppermute x8, waiting for transfers between devices, with_halo(): lax.ppermute(head, axis, [((i + 1) % count, i) for i in range(count)])  26.2 us
    ppermute x8, waiting for transfers between devices, with_halo(): lax.ppermute(tail, axis, [(i, (i + 1) % count) for i in range(count)])  21.5 us
    add x4, other arithmetic, advance(): center + TIME_STEP * velocity * advect + DIFFUSE * (lap_x + lap_z)  18 us
    dot_general x4, matrix products, advance(): jnp.dot(flattened, table_t, precision=lax.Precision.HIGHEST, preferred_el...  12.1 us
    slice x4, other arithmetic, advance(): explicit[:1]  9.38 us
    ppermute x8, starting transfers between devices, with_halo(): lax.ppermute(tail, axis, [(i, (i + 1) % count) for i in range(count)])  6.64 us
  transfers between devices with their start and end apart: 17, of which 17 were waited for; matrix products, arithmetic and copies ran while one was open for 0% of the time, Pallas kernels for 0%

profile of v1, /device:TPU:22, one launch (start us, length us, event | category | flops | bytes accessed | tf_op | source)
XLA Modules:
  0.0 224.7 jit_solution(7545264665241350106)
XLA Ops:
  0.0 0.3 collective-permute-start
  0.3 73.3 %collective-permute-done = f32[1,3,64,16,256]{4,3,2,1,0:T(8,128)S(1)} collective-permute-done((f32[1,3,64,16,256]{4,3,2,1,0:T(8,128)}, f32[1,3,64,16,256]{4,3,2,1,0:T(8,128)S(1)}, u32[]{:S(2)}, u32[]{:S(2)}) %collective-permute-start) | collective-permute-done | bytes 3145760 | tf_op jit(solution)/shard_map/ppermute | solution.py:34
  73.7 5.4 %fusion.39 = (f32[]{:T(128)}, f32[]{:T(128)}) fusion(f32[1,3,64,16,256]{4,3,2,1,0:T(8,128)} %param.8, f32[1,3,64,16,256]{4,3,2,1,0:T(8,128)S(1)} %collective-permute-done, f32[1,3,64,16,256]{4,3,2,1,0:T(8,128)} %param.7), kind=kLoop, calls=%fused_computation.85 | loop fusion | flops 3932158 | bytes 9437192 | tf_op jit(solution)/shard_map/reduce_sum | solution.py:100
  79.1 28.6 %all-reduce = (f32[]{:T(128)}, f32[]{:T(128)}) all-reduce(f32[]{:T(128)} %get-tuple-element.6, f32[]{:T(128)} %get-tuple-element.5), channel_id=1, replica_groups=mesh['seg'=8,'gx'=2,'gz'=16] {'gz'}, use_global_device_ids=true, to_apply=%region_1.0 | all-reduce | flops 2 | bytes 16 | tf_op jit(solution)/shard_map/psum | solution.py:100
  107.7 5.6 %all-reduce.1 = (f32[]{:T(128)}, f32[]{:T(128)}) all-reduce(f32[]{:T(128)} %get-tuple-element.7, f32[]{:T(128)} %get-tuple-element.8), channel_id=1, replica_groups=mesh['seg'=8,'gx'=2,'gz'=16] {'gx'}, use_global_device_ids=true, to_apply=%region_2.0 | all-reduce | flops 2 | bytes 16 | tf_op jit(solution)/shard_map/psum | solution.py:99
  114.5 4.0 %fusion.40 = f32[3,64,16,256]{3,2,1,0:T(8,128)S(1)} fusion(f32[1,3,64,16,256]{4,3,2,1,0:T(8,128)S(1)} %copy-done, f32[]{:T(128)S(6)} %div.31, f32[1,3,64,16,256]{4,3,2,1,0:T(8,128)} %copy-done.1, f32[1,3,64,16,256]{4,3,2,1,0:T(8,128)} %param.7), kind=kLoop, calls=%fused_computation.86 | loop fusion | flops 2359296 | bytes 12582916 | tf_op jit(solution)/shard_map/sub | solution.py:103
  118.6 1.4 collective-permute-start.1
  120.0 0.7 collective-permute-start.2
  120.7 2.6 %collective-permute-done.1 = f32[3,2,16,256]{3,2,1,0:T(8,128)S(1)} collective-permute-done((f32[3,2,16,256]{3,2,1,0:T(8,128)S(1)}, f32[3,2,16,256]{3,2,1,0:T(8,128)S(1)}, u32[]{:S(2)}, u32[]{:S(2)}) %collective-permute-start.1) | collective-permute-done | bytes 98336 | tf_op jit(solution)/shard_map/ppermute | solution.py:22
  123.3 1.3 collective-permute-done.2
  124.6 0.3 pad_maximum_fusion.26
  124.9 0.0 collective-permute-start.3
  124.9 0.5 collective-permute-start.4
  125.4 5.0 %collective-permute-done.3 = f32[3,68,2,256]{3,2,1,0:T(2,128)S(1)} collective-permute-done((f32[3,68,2,256]{3,2,1,0:T(2,128)S(1)}, f32[3,68,2,256]{3,2,1,0:T(2,128)S(1)}, u32[]{:S(2)}, u32[]{:S(2)}) %collective-permute-start.3) | collective-permute-done | bytes 417824 | tf_op jit(solution)/shard_map/ppermute | solution.py:24
  130.4 3.1 %collective-permute-done.4 = f32[3,68,2,256]{3,2,1,0:T(2,128)S(1)} collective-permute-done((f32[3,68,2,256]{3,2,1,0:T(2,128)S(1)}, f32[3,68,2,256]{3,2,1,0:T(2,128)S(1)}, u32[]{:S(2)}, u32[]{:S(2)}) %collective-permute-start.4) | collective-permute-done | bytes 417824 | tf_op jit(solution)/shard_map/ppermute | solution.py:22
  133.6 1.3 pad_maximum_fusion
  134.9 4.1 %fusion.30 = f32[3,64,16,256]{3,2,1,0:T(8,128)} fusion(f32[3,68,18,256]{3,2,1,0:T(8,128)S(1)} %get-tuple-element.24, f32[3,68,18,256]{3,2,1,0:T(8,128)S(1)} %get-tuple-element.23, f32[3,64,16,256]{3,2,1,0:T(8,128)S(1)} %fusion.40, f32[3,2,16,256]{3,2,1,0:T(8,128)S(1)} %collective-permute-done.2, f32[3,2,16,256]{3,2,1,0:T(8,128)S(1)} %collective-permute-done.1, ...), kind=kLoop, calls=%fused_computation.67 | loop fusion | flops 18874368 | bytes 19072000 | tf_op jit(solution)/shard_map/add | solution.py:78
  139.0 2.3 %fusion.52 = (f32[1,64,16,256]{3,2,1,0:T(8,128)S(1)}, f32[1,64,16,256]{3,2,1,0:T(8,128)S(1)}, f32[1,64,16,256]{3,2,1,0:T(8,128)S(1)}) fusion(f32[3,64,16,256]{3,2,1,0:T(8,128)} %fusion.30, f32[3,64,16,256]{3,2,1,0:T(8,128)S(1)} %fusion.40, f32[256]{0:T(256)S(1)} %broadcast_multiply_fusion), kind=kLoop, calls=%fused_computation.114 | loop fusion | flops 524288 | bytes 7341056 | tf_op jit(solution)/shard_map/slice | solution.py:80
  141.3 0.3 pad_maximum_fusion.12
  141.6 0.6 copy-done.2
  142.3 2.6 %fusion.54 = f32[3072,256]{1,0:T(8,128)S(1)} fusion(f32[3072,256]{1,0:T(8,128)S(1)} %bitcast.47, f32[256,256]{1,0:T(8,128)S(1)} %copy-done.2), kind=kOutput, calls=%fused_computation.116 | convolution fusion | flops 2415919104 | bytes 6553600 | tf_op jit(solution)/shard_map/dot_general | solution.py:83
  144.9 1.1 collective-permute-start.5
  146.1 1.0 collective-permute-start.6
  147.0 2.6 %collective-permute-done.5 = f32[3,2,16,256]{3,2,1,0:T(8,128)S(1)} collective-permute-done((f32[3,2,16,256]{3,2,1,0:T(8,128)S(1)}, f32[3,2,16,256]{3,2,1,0:T(8,128)S(1)}, u32[]{:S(2)}, u32[]{:S(2)}) %collective-permute-start.5) | collective-permute-done | bytes 98336 | tf_op jit(solution)/shard_map/ppermute | solution.py:22
  149.6 1.1 collective-permute-done.6
  150.7 0.3 pad_maximum_fusion.23
  151.0 0.0 collective-permute-start.7
  151.0 0.5 collective-permute-start.8
  151.5 0.1 slice.326
  151.6 5.0 %collective-permute-done.7 = f32[3,68,2,256]{3,2,1,0:T(2,128)S(1)} collective-permute-done((f32[3,68,2,256]{3,2,1,0:T(2,128)S(1)}, f32[3,68,2,256]{3,2,1,0:T(2,128)S(1)}, u32[]{:S(2)}, u32[]{:S(2)}) %collective-permute-start.7) | collective-permute-done | bytes 417824 | tf_op jit(solution)/shard_map/ppermute | solution.py:24
  156.6 3.1 %collective-permute-done.8 = f32[3,68,2,256]{3,2,1,0:T(2,128)S(1)} collective-permute-done((f32[3,68,2,256]{3,2,1,0:T(2,128)S(1)}, f32[3,68,2,256]{3,2,1,0:T(2,128)S(1)}, u32[]{:S(2)}, u32[]{:S(2)}) %collective-permute-start.8) | collective-permute-done | bytes 417824 | tf_op jit(solution)/shard_map/ppermute | solution.py:22
  159.7 1.3 pad_maximum_fusion.1
  161.0 5.0 %fusion.24 = f32[3,64,16,256]{3,2,1,0:T(8,128)} fusion(f32[3,68,18,256]{3,2,1,0:T(8,128)S(1)} %get-tuple-element.20, f32[3,68,18,256]{3,2,1,0:T(8,128)S(1)} %get-tuple-element.19, f32[3,64,16,256]{3,2,1,0:T(8,128)S(1)} %bitcast.41, f32[3,2,16,256]{3,2,1,0:T(8,128)} %copy-done.3, f32[3,2,16,256]{3,2,1,0:T(8,128)S(1)} %collective-permute-done.5, ...), kind=kLoop, calls=%fused_computation.57 | loop fusion | flops 18874368 | bytes 19072000 | tf_op jit(solution)/shard_map/add | solution.py:78
  166.0 2.3 %fusion.50 = (f32[1,64,16,256]{3,2,1,0:T(8,128)S(1)}, f32[1,64,16,256]{3,2,1,0:T(8,128)S(1)}, f32[1,64,16,256]{3,2,1,0:T(8,128)S(1)}) fusion(f32[3,64,16,256]{3,2,1,0:T(8,128)} %fusion.24, f32[1,64,16,256]{3,2,1,0:T(8,128)S(1)} %bitcast.50, f32[256]{0:T(256)S(1)} %broadcast_multiply_fusion), kind=kLoop, calls=%fused_computation.112 | loop fusion | flops 524288 | bytes 7341056 | tf_op jit(solution)/shard_map/slice | solution.py:80
  168.3 0.3 pad_maximum_fusion.13
  168.6 2.6 %fusion.55 = f32[3072,256]{1,0:T(8,128)S(1)} fusion(f32[3072,256]{1,0:T(8,128)S(1)} %bitcast.48, f32[256,256]{1,0:T(8,128)S(1)} %copy-done.2), kind=kOutput, calls=%fused_computation.117 | convolution fusion | flops 2415919104 | bytes 6553600 | tf_op jit(solution)/shard_map/dot_general | solution.py:83
  171.3 1.3 collective-permute-start.10
  172.6 0.8 collective-permute-start.9
  173.4 2.6 %collective-permute-done.10 = f32[3,2,16,256]{3,2,1,0:T(8,128)S(1)} collective-permute-done((f32[3,2,16,256]{3,2,1,0:T(8,128)S(1)}, f32[3,2,16,256]{3,2,1,0:T(8,128)S(1)}, u32[]{:S(2)}, u32[]{:S(2)}) %collective-permute-start.10) | collective-permute-done | bytes 98336 | tf_op jit(solution)/shard_map/ppermute | solution.py:24
  176.0 1.2 collective-permute-done.9
  177.2 0.3 pad_maximum_fusion.20
  177.5 0.0 collective-permute-start.11
  177.5 0.5 collective-permute-start.12
  178.0 0.1 slice.340
  178.1 5.0 %collective-permute-done.11 = f32[3,68,2,256]{3,2,1,0:T(2,128)S(1)} collective-permute-done((f32[3,68,2,256]{3,2,1,0:T(2,128)S(1)}, f32[3,68,2,256]{3,2,1,0:T(2,128)S(1)}, u32[]{:S(2)}, u32[]{:S(2)}) %collective-permute-start.11) | collective-permute-done | bytes 417824 | tf_op jit(solution)/shard_map/ppermute | solution.py:24
  183.1 3.1 %collective-permute-done.12 = f32[3,68,2,256]{3,2,1,0:T(2,128)S(1)} collective-permute-done((f32[3,68,2,256]{3,2,1,0:T(2,128)S(1)}, f32[3,68,2,256]{3,2,1,0:T(2,128)S(1)}, u32[]{:S(2)}, u32[]{:S(2)}) %collective-permute-start.12) | collective-permute-done | bytes 417824 | tf_op jit(solution)/shard_map/ppermute | solution.py:22
  186.2 1.3 pad_maximum_fusion.2
  187.5 4.9 %fusion.18 = f32[3,64,16,256]{3,2,1,0:T(8,128)} fusion(f32[3,68,18,256]{3,2,1,0:T(8,128)S(1)} %get-tuple-element.16, f32[3,68,18,256]{3,2,1,0:T(8,128)S(1)} %get-tuple-element.15, f32[3,64,16,256]{3,2,1,0:T(8,128)S(1)} %bitcast.45, f32[3,2,16,256]{3,2,1,0:T(8,128)S(1)} %collective-permute-done.10, f32[3,2,16,256]{3,2,1,0:T(8,128)} %copy-done.4, ...), kind=kLoop, calls=%fused_computation.47 | loop fusion | flops 18874368 | bytes 19072000 | tf_op jit(solution)/shard_map/add | solution.py:78
  192.4 2.3 %fusion.48 = (f32[1,64,16,256]{3,2,1,0:T(8,128)S(1)}, f32[1,64,16,256]{3,2,1,0:T(8,128)S(1)}, f32[1,64,16,256]{3,2,1,0:T(8,128)S(1)}) fusion(f32[3,64,16,256]{3,2,1,0:T(8,128)} %fusion.18, f32[1,64,16,256]{3,2,1,0:T(8,128)S(1)} %bitcast.51, f32[256]{0:T(256)S(1)} %broadcast_multiply_fusion), kind=kLoop, calls=%fused_computation.110 | loop fusion | flops 524288 | bytes 7341056 | tf_op jit(solution)/shard_map/slice | solution.py:80
  194.7 0.3 pad_maximum_fusion.14
  195.1 2.6 %fusion.56 = f32[3072,256]{1,0:T(8,128)S(1)} fusion(f32[3072,256]{1,0:T(8,128)S(1)} %bitcast.46, f32[256,256]{1,0:T(8,128)S(1)} %copy-done.2), kind=kOutput, calls=%fused_computation.118 | convolution fusion | flops 2415919104 | bytes 6553600 | tf_op jit(solution)/shard_map/dot_general | solution.py:83
  197.7 1.3 collective-permute-start.13
  199.0 0.8 collective-permute-start.14
  199.8 2.6 %collective-permute-done.13 = f32[3,2,16,256]{3,2,1,0:T(8,128)S(1)} collective-permute-done((f32[3,2,16,256]{3,2,1,0:T(8,128)S(1)}, f32[3,2,16,256]{3,2,1,0:T(8,128)S(1)}, u32[]{:S(2)}, u32[]{:S(2)}) %collective-permute-start.13) | collective-permute-done | bytes 98336 | tf_op jit(solution)/shard_map/ppermute | solution.py:22
  202.4 1.2 collective-permute-done.14
  203.7 0.3 pad_maximum_fusion.17
  204.0 0.5 collective-permute-start.16
  204.5 0.1 slice.354
  204.5 5.0 %collective-permute-done.15 = f32[3,68,2,256]{3,2,1,0:T(2,128)S(1)} collective-permute-done((f32[3,68,2,256]{3,2,1,0:T(2,128)S(1)}, f32[3,68,2,256]{3,2,1,0:T(2,128)S(1)}, u32[]{:S(2)}, u32[]{:S(2)}) %collective-permute-start.15) | collective-permute-done | bytes 417824 | tf_op jit(solution)/shard_map/ppermute | solution.py:24
  209.5 3.1 %collective-permute-done.16 = f32[3,68,2,256]{3,2,1,0:T(2,128)S(1)} collective-permute-done((f32[3,68,2,256]{3,2,1,0:T(2,128)S(1)}, f32[3,68,2,256]{3,2,1,0:T(2,128)S(1)}, u32[]{:S(2)}, u32[]{:S(2)}) %collective-permute-start.16) | collective-permute-done | bytes 417824 | tf_op jit(solution)/shard_map/ppermute | solution.py:22
  212.7 1.3 pad_maximum_fusion.3
  214.0 4.1 %fusion.12 = f32[3,64,16,256]{3,2,1,0:T(8,128)} fusion(f32[3,68,18,256]{3,2,1,0:T(8,128)S(1)} %get-tuple-element.12, f32[3,68,18,256]{3,2,1,0:T(8,128)S(1)} %get-tuple-element.11, f32[3,64,16,256]{3,2,1,0:T(8,128)S(1)} %bitcast.37, f32[3,2,16,256]{3,2,1,0:T(8,128)S(1)} %collective-permute-done.14, f32[3,2,16,256]{3,2,1,0:T(8,128)S(1)} %collective-permute-done.13, ...), kind=kLoop, calls=%fused_computation.37 | loop fusion | flops 18874368 | bytes 19072000 | tf_op jit(solution)/shard_map/add | solution.py:78
  218.1 2.4 %fusion.46 = (f32[1,64,16,256]{3,2,1,0:T(8,128)S(1)}, f32[1,64,16,256]{3,2,1,0:T(8,128)S(1)}, f32[1,64,16,256]{3,2,1,0:T(8,128)S(1)}) fusion(f32[3,64,16,256]{3,2,1,0:T(8,128)} %fusion.12, f32[1,64,16,256]{3,2,1,0:T(8,128)S(1)} %bitcast.49, f32[256]{0:T(256)S(1)} %broadcast_multiply_fusion), kind=kLoop, calls=%fused_computation.108 | loop fusion | flops 524288 | bytes 7341056 | tf_op jit(solution)/shard_map/slice | solution.py:80
  220.5 4.3 %fusion.41 = f32[1,3,64,16,256]{4,3,2,1,0:T(8,128)} fusion(f32[256,256,1,1]{1,0,3,2:T(8,128)S(1)} %copy-done.5, f32[1,64,16,256]{3,2,1,0:T(8,128)S(1)} %get-tuple-element.28, f32[1,64,16,256]{3,2,1,0:T(8,128)S(1)} %get-tuple-element.29, f32[1,64,16,256]{3,2,1,0:T(8,128)S(1)} %get-tuple-element.27), kind=kOutput, calls=%fused_computation.87 | convolution fusion | flops 2417491968 | bytes 6553600 | tf_op jit(solution)/shard_map/dot_general | solution.py:83
  (22 shorter events, 0.1 us)
Async XLA Ops:
  0.0 114.5 %copy-start = (f32[1,3,64,16,256]{4,3,2,1,0:T(8,128)S(1)}, f32[1,3,64,16,256]{4,3,2,1,0:T(8,128)}, u32[]{:S(2)}) copy-start(f32[1,3,64,16,256]{4,3,2,1,0:T(8,128)} %param.8) | copy-start | bytes 9437188
  0.0 73.7 %collective-permute-start = (f32[1,3,64,16,256]{4,3,2,1,0:T(8,128)}, f32[1,3,64,16,256]{4,3,2,1,0:T(8,128)S(1)}, u32[]{:S(2)}, u32[]{:S(2)}) collective-permute-start(f32[1,3,64,16,256]{4,3,2,1,0:T(8,128)} %param.6), channel_id=1, source_target_pairs={{0,224},{32,0},{64,32},{96,64},{128,96},{160,128},{192,160},{224,1... | collective-permute-start | bytes 9437192 | tf_op jit(solution)/shard_map/ppermute | solution.py:34
  73.7 5.4 %copy-start.1 = (f32[1,3,64,16,256]{4,3,2,1,0:T(8,128)}, f32[1,3,64,16,256]{4,3,2,1,0:T(8,128)S(1)}, u32[]{:S(2)}) copy-start(f32[1,3,64,16,256]{4,3,2,1,0:T(8,128)S(1)} %collective-permute-done) | copy-start | bytes 9437188
  118.5 6.9 %copy-start.6 = (f32[256]{0:T(256)S(1)}, f32[256]{0:T(256)}, u32[]{:S(2)}) copy-start(f32[256]{0:T(256)} %param.9) | copy-start | bytes 3076
  118.5 6.9 %copy-start.7 = (f32[256]{0:T(256)S(1)}, f32[256]{0:T(256)}, u32[]{:S(2)}) copy-start(f32[256]{0:T(256)} %param.10) | copy-start | bytes 3076
  118.6 4.7 %collective-permute-start.1 = (f32[3,2,16,256]{3,2,1,0:T(8,128)S(1)}, f32[3,2,16,256]{3,2,1,0:T(8,128)S(1)}, u32[]{:S(2)}, u32[]{:S(2)}) collective-permute-start(f32[3,2,16,256]{3,2,1,0:T(8,128)S(1)} %get-tuple-element.45), channel_id=1, source_target_pairs={{0,16},{16,0},{1,17},{17,1},{2,18},{18,2},{3,19},{19,3},{4,20},{20... | collective-permute-start | bytes 294920 | tf_op jit(solution)/shard_map/ppermute | solution.py:22
  120.0 4.6 %collective-permute-start.2 = (f32[3,2,16,256]{3,2,1,0:T(8,128)S(1)}, f32[3,2,16,256]{3,2,1,0:T(8,128)S(1)}, u32[]{:S(2)}, u32[]{:S(2)}) collective-permute-start(f32[3,2,16,256]{3,2,1,0:T(8,128)S(1)} %get-tuple-element.46), channel_id=1, source_target_pairs={{16,0},{0,16},{17,1},{1,17},{18,2},{2,18},{19,3},{3,19},{20,4},{4,... | collective-permute-start | bytes 294920 | tf_op jit(solution)/shard_map/ppermute | solution.py:24
  124.9 5.6 %collective-permute-start.3 = (f32[3,68,2,256]{3,2,1,0:T(2,128)S(1)}, f32[3,68,2,256]{3,2,1,0:T(2,128)S(1)}, u32[]{:S(2)}, u32[]{:S(2)}) collective-permute-start(f32[3,68,2,256]{3,2,1,0:T(2,128)S(1)} %get-tuple-element.25), channel_id=1, source_target_pairs={{1,0},{2,1},{3,2},{4,3},{5,4},{6,5},{7,6},{8,7},{9,8},{10,9},{11,1... | collective-permute-start | bytes 1253384 | tf_op jit(solution)/shard_map/ppermute | solution.py:24
  124.9 8.7 %collective-permute-start.4 = (f32[3,68,2,256]{3,2,1,0:T(2,128)S(1)}, f32[3,68,2,256]{3,2,1,0:T(2,128)S(1)}, u32[]{:S(2)}, u32[]{:S(2)}) collective-permute-start(f32[3,68,2,256]{3,2,1,0:T(2,128)S(1)} %get-tuple-element.26), channel_id=1, source_target_pairs={{0,1},{1,2},{2,3},{3,4},{4,5},{5,6},{6,7},{7,8},{8,9},{9,10},{10,1... | collective-permute-start | bytes 1253384 | tf_op jit(solution)/shard_map/ppermute | solution.py:22
  141.3 1.0 copy-start.2
  144.9 4.7 %collective-permute-start.5 = (f32[3,2,16,256]{3,2,1,0:T(8,128)S(1)}, f32[3,2,16,256]{3,2,1,0:T(8,128)S(1)}, u32[]{:S(2)}, u32[]{:S(2)}) collective-permute-start(f32[3,2,16,256]{3,2,1,0:T(8,128)S(1)} %get-tuple-element.40), channel_id=1, source_target_pairs={{0,16},{16,0},{1,17},{17,1},{2,18},{18,2},{3,19},{19,3},{4,20},{20... | collective-permute-start | bytes 294920 | tf_op jit(solution)/shard_map/ppermute | solution.py:22
  146.1 4.6 %collective-permute-start.6 = (f32[3,2,16,256]{3,2,1,0:T(8,128)S(1)}, f32[3,2,16,256]{3,2,1,0:T(8,128)S(1)}, u32[]{:S(2)}, u32[]{:S(2)}) collective-permute-start(f32[3,2,16,256]{3,2,1,0:T(8,128)S(1)} %get-tuple-element.41), channel_id=1, source_target_pairs={{16,0},{0,16},{17,1},{1,17},{18,2},{2,18},{19,3},{3,19},{20,4},{4,... | collective-permute-start | bytes 294920 | tf_op jit(solution)/shard_map/ppermute | solution.py:24
  150.7 10.3 %copy-start.3 = (f32[3,2,16,256]{3,2,1,0:T(8,128)}, f32[3,2,16,256]{3,2,1,0:T(8,128)S(1)}, u32[]{:S(2)}) copy-start(f32[3,2,16,256]{3,2,1,0:T(8,128)S(1)} %collective-permute-done.6) | copy-start | bytes 294916
  151.0 5.6 %collective-permute-start.7 = (f32[3,68,2,256]{3,2,1,0:T(2,128)S(1)}, f32[3,68,2,256]{3,2,1,0:T(2,128)S(1)}, u32[]{:S(2)}, u32[]{:S(2)}) collective-permute-start(f32[3,68,2,256]{3,2,1,0:T(2,128)S(1)} %get-tuple-element.21), channel_id=1, source_target_pairs={{1,0},{2,1},{3,2},{4,3},{5,4},{6,5},{7,6},{8,7},{9,8},{10,9},{11,1... | collective-permute-start | bytes 1253384 | tf_op jit(solution)/shard_map/ppermute | solution.py:24
  151.0 8.7 %collective-permute-start.8 = (f32[3,68,2,256]{3,2,1,0:T(2,128)S(1)}, f32[3,68,2,256]{3,2,1,0:T(2,128)S(1)}, u32[]{:S(2)}, u32[]{:S(2)}) collective-permute-start(f32[3,68,2,256]{3,2,1,0:T(2,128)S(1)} %get-tuple-element.22), channel_id=1, source_target_pairs={{0,1},{1,2},{2,3},{3,4},{4,5},{5,6},{6,7},{7,8},{8,9},{9,10},{10,1... | collective-permute-start | bytes 1253384 | tf_op jit(solution)/shard_map/ppermute | solution.py:22
  171.3 4.7 %collective-permute-start.10 = (f32[3,2,16,256]{3,2,1,0:T(8,128)S(1)}, f32[3,2,16,256]{3,2,1,0:T(8,128)S(1)}, u32[]{:S(2)}, u32[]{:S(2)}) collective-permute-start(f32[3,2,16,256]{3,2,1,0:T(8,128)S(1)} %get-tuple-element.36), channel_id=1, source_target_pairs={{16,0},{0,16},{17,1},{1,17},{18,2},{2,18},{19,3},{3,19},{20,4},{4,... | collective-permute-start | bytes 294920 | tf_op jit(solution)/shard_map/ppermute | solution.py:24
  172.6 4.6 %collective-permute-start.9 = (f32[3,2,16,256]{3,2,1,0:T(8,128)S(1)}, f32[3,2,16,256]{3,2,1,0:T(8,128)S(1)}, u32[]{:S(2)}, u32[]{:S(2)}) collective-permute-start(f32[3,2,16,256]{3,2,1,0:T(8,128)S(1)} %get-tuple-element.35), channel_id=1, source_target_pairs={{0,16},{16,0},{1,17},{17,1},{2,18},{18,2},{3,19},{19,3},{4,20},{20... | collective-permute-start | bytes 294920 | tf_op jit(solution)/shard_map/ppermute | solution.py:22
  177.2 10.3 %copy-start.4 = (f32[3,2,16,256]{3,2,1,0:T(8,128)}, f32[3,2,16,256]{3,2,1,0:T(8,128)S(1)}, u32[]{:S(2)}) copy-start(f32[3,2,16,256]{3,2,1,0:T(8,128)S(1)} %collective-permute-done.9) | copy-start | bytes 294916
  177.5 5.6 %collective-permute-start.11 = (f32[3,68,2,256]{3,2,1,0:T(2,128)S(1)}, f32[3,68,2,256]{3,2,1,0:T(2,128)S(1)}, u32[]{:S(2)}, u32[]{:S(2)}) collective-permute-start(f32[3,68,2,256]{3,2,1,0:T(2,128)S(1)} %get-tuple-element.17), channel_id=1, source_target_pairs={{1,0},{2,1},{3,2},{4,3},{5,4},{6,5},{7,6},{8,7},{9,8},{10,9},{11,1... | collective-permute-start | bytes 1253384 | tf_op jit(solution)/shard_map/ppermute | solution.py:24
  177.5 8.7 %collective-permute-start.12 = (f32[3,68,2,256]{3,2,1,0:T(2,128)S(1)}, f32[3,68,2,256]{3,2,1,0:T(2,128)S(1)}, u32[]{:S(2)}, u32[]{:S(2)}) collective-permute-start(f32[3,68,2,256]{3,2,1,0:T(2,128)S(1)} %get-tuple-element.18), channel_id=1, source_target_pairs={{0,1},{1,2},{2,3},{3,4},{4,5},{5,6},{6,7},{7,8},{8,9},{9,10},{10,1... | collective-permute-start | bytes 1253384 | tf_op jit(solution)/shard_map/ppermute | solution.py:22
  197.7 4.7 %collective-permute-start.13 = (f32[3,2,16,256]{3,2,1,0:T(8,128)S(1)}, f32[3,2,16,256]{3,2,1,0:T(8,128)S(1)}, u32[]{:S(2)}, u32[]{:S(2)}) collective-permute-start(f32[3,2,16,256]{3,2,1,0:T(8,128)S(1)} %get-tuple-element.30), channel_id=1, source_target_pairs={{0,16},{16,0},{1,17},{17,1},{2,18},{18,2},{3,19},{19,3},{4,20},{20... | collective-permute-start | bytes 294920 | tf_op jit(solution)/shard_map/ppermute | solution.py:22
  199.0 4.6 %collective-permute-start.14 = (f32[3,2,16,256]{3,2,1,0:T(8,128)S(1)}, f32[3,2,16,256]{3,2,1,0:T(8,128)S(1)}, u32[]{:S(2)}, u32[]{:S(2)}) collective-permute-start(f32[3,2,16,256]{3,2,1,0:T(8,128)S(1)} %get-tuple-element.31), channel_id=1, source_target_pairs={{16,0},{0,16},{17,1},{1,17},{18,2},{2,18},{19,3},{3,19},{20,4},{4,... | collective-permute-start | bytes 294920 | tf_op jit(solution)/shard_map/ppermute | solution.py:24
  203.9 5.6 %collective-permute-start.15 = (f32[3,68,2,256]{3,2,1,0:T(2,128)S(1)}, f32[3,68,2,256]{3,2,1,0:T(2,128)S(1)}, u32[]{:S(2)}, u32[]{:S(2)}) collective-permute-start(f32[3,68,2,256]{3,2,1,0:T(2,128)S(1)} %get-tuple-element.13), channel_id=1, source_target_pairs={{1,0},{2,1},{3,2},{4,3},{5,4},{6,5},{7,6},{8,7},{9,8},{10,9},{11,1... | collective-permute-start | bytes 1253384 | tf_op jit(solution)/shard_map/ppermute | solution.py:24
  204.0 8.7 %collective-permute-start.16 = (f32[3,68,2,256]{3,2,1,0:T(2,128)S(1)}, f32[3,68,2,256]{3,2,1,0:T(2,128)S(1)}, u32[]{:S(2)}, u32[]{:S(2)}) collective-permute-start(f32[3,68,2,256]{3,2,1,0:T(2,128)S(1)} %get-tuple-element.14), channel_id=1, source_target_pairs={{0,1},{1,2},{2,3},{3,4},{4,5},{5,6},{6,7},{7,8},{8,9},{9,10},{10,1... | collective-permute-start | bytes 1253384 | tf_op jit(solution)/shard_map/ppermute | solution.py:22
  218.1 2.4 %copy-start.5 = (f32[256,256,1,1]{1,0,3,2:T(8,128)S(1)}, f32[256,256,1,1]{1,0,3,2:T(8,128)}, u32[]{:S(2)}) copy-start(f32[256,256,1,1]{1,0,3,2:T(8,128)} %constant.40) | copy-start | bytes 786436
